TPU v7x, 32 devices: a whole 2x2x4 slice. The times are simulated.
32 devices in a mesh: groups: 2 (over x), track: 4 (over y, core), frame: 4 (over z).
Axes of the slice: x: 2, y: 2, z: 4, core: 2. Of those that a mesh axis runs over, the one named last changes fastest.
Arguments:
- frames: bfloat16 [16, 4096, 256], P(('groups', 'frame')), parts along dimension 0, may hold values from -9 to 9
- query_frame: int32 [1024], P(('groups', 'track')), parts along dimension 0, may hold values from 0 to 7
- query_pixel: int32 [1024], P(('groups', 'track')), parts along dimension 0, may hold values from 0 to 4095
- cotangent: float32 [2, 16, 512], P(None, ('groups', 'frame'), 'track'), parts along dimension 1, may hold values from -48 to 48
Outputs:
- frame_grad: float32 [4096, 16, 256], P('track', ('groups', 'frame')), parts along dimension 1
- query_grad: float32 [1024, 256], P(('groups', 'track', 'frame')), parts along dimension 0
There are 2 independent parts, one for each index of `groups`. A program takes and returns all parts, laid end to end along the dimension named above; each array names one. Nothing has to cross between parts.
All inputs are finite; a program needn't handle non-finite values.
Results may differ from a plain program's by a relative error of at most 0.0029.
Values may be sent and summed in bfloat16 or wider, within the bound.
No kernel may reach another device: no remote copies, remote signals or barrier semaphores. Data moves between devices by JAX's collectives and lax.ppermute only.
A program may use at most 64 MiB of HBM per device.

v0:
```python
import jax
import jax.numpy as jnp
from jax import lax
from jax.sharding import PartitionSpec as P

C = 256
FEAT_H = 64
FEAT_W = 64


def on_device(frames, query_frame, query_pixel, cotangent):
    held_frames = frames.shape[0]
    pixels = frames.shape[1]
    channels = frames.shape[2]
    offset = lax.axis_index("frame") * held_frames
    local_index = query_frame - offset
    inside = (local_index >= 0) & (local_index < held_frames)
    row_index = jnp.clip(local_index, 0, held_frames - 1) * pixels + query_pixel
    picked = frames.reshape(held_frames * pixels, channels)[row_index]
    picked = jnp.where(inside[:, None], picked.astype(jnp.float32), 0.0)
    query_feat = lax.psum(picked.astype(jnp.bfloat16), "frame")
    score_scale = C ** (-0.5)
    pixel_ids = jnp.arange(pixels)
    coord_x = (pixel_ids % FEAT_W * (2.0 / (FEAT_W - 1)) - 1.0).astype(jnp.float32)
    coord_y = (pixel_ids // FEAT_W * (2.0 / (FEAT_H - 1)) - 1.0).astype(jnp.float32)
    scores = (
        jnp.einsum("qc,tpc->tqp", query_feat, frames, preferred_element_type=jnp.float32)
        * score_scale
    )
    peak_score = jnp.max(scores, axis=2, keepdims=True)
    exp_scores = jnp.exp(scores - peak_score)
    weights = exp_scores / jnp.sum(exp_scores, axis=2, keepdims=True)
    expect_x = jnp.sum(weights * coord_x, axis=2)
    expect_y = jnp.sum(weights * coord_y, axis=2)
    grad_x = cotangent[0]
    grad_y = cotangent[1]
    inner_sum = grad_x * expect_x + grad_y * expect_y
    cost_grad = (
        weights
        * (grad_x[:, :, None] * coord_x + grad_y[:, :, None] * coord_y - inner_sum[:, :, None])
        * score_scale
    ).astype(jnp.bfloat16)
    query_term = jnp.einsum("tqp,tpc->qc", cost_grad, frames, preferred_element_type=jnp.float32)
    query_grad = lax.psum_scatter(query_term, "frame", scatter_dimension=0, tiled=True)
    everyone = lax.all_gather(query_feat, "track", axis=0, tiled=True)
    frame_grad = jnp.einsum(
        "tqp,qc->ptc",
        lax.all_to_all(cost_grad, "track", split_axis=2, concat_axis=1, tiled=True),
        everyone,
        preferred_element_type=jnp.float32,
    )
    return (frame_grad, query_grad)


def solution(mesh):
    return jax.shard_map(
        on_device,
        mesh=mesh,
        in_specs=(
            P(("groups", "frame"), None, None),
            P(("groups", "track")),
            P(("groups", "track")),
            P(None, ("groups", "frame"), "track"),
        ),
        out_specs=(P("track", ("groups", "frame"), None), P(("groups", "track", "frame"), None)),
        check_vma=False,
    )
```

profile of v0, /device:TPU:0, one launch (start us, length us, event | category | flops | bytes accessed | tf_op | source)
XLA Modules:
  0.0 114.3 jit_solution(15682147279452416401)
XLA Ops:
  7.2 0.0 all-reduce.2.cloned.1.call-start
  7.2 0.7 compare_and_fusion
  7.9 0.7 compare_select_fusion
  8.6 3.5 %gather_fusion = bf16[128,256]{1,0:T(8,128)(2,1)S(1)} fusion(bf16[8192,256]{1,0:T(8,128)(2,1)} %bitcast.38, s32[1024]{0:T(1024)S(1)} %pad_clamp_fusion), kind=kCustom, calls=%fused_computation | custom fusion | bytes 131584 | tf_op jit(solution)/shard_map/gather | solution.py:19
  12.1 0.7 select_convert_fusion
  12.8 0.0 all-reduce.2.cloned.1.call-update
  12.8 0.7 slice_bitcast_fusion.1
  13.5 36.5 %all-reduce.2.cloned.1.call-done = bf16[128,256]{1,0:T(8,128)(2,1)} async-done(((bf16[128,256]{1,0:T(8,128)(2,1)}), bf16[128,256]{1,0:T(8,128)(2,1)}) %all-reduce.2.cloned.1.call-update) | async-done | bytes 65552 | tf_op jit(solution)/shard_map/psum | solution.py:21
  50.0 0.0 copy-start.1
  50.0 7.0 %multiply_reduce_fusion.1 = (f32[2,128]{1,0:T(2,128)S(1)}, f32[2,128]{1,0:T(2,128)S(1)}, f32[2,128,4096]{2,1,0:T(8,128)}) fusion(f32[4096]{0:T(1024)S(1)} %get-tuple-element.11, f32[4096]{0:T(1024)S(1)} %get-tuple-element.12, bf16[2,4096,256]{2,1,0:T(8,128)(2,1)} %param.4, bf16[128,256]{1,0:T(8,128)(2,1)} %all-reduce.2.cloned.1.call-done), kind=kOutput, calls=%fused_computation.10 | convolution fusion | flops 544219136 | bytes 8488960 | tf_op jit(solution)/shard_map/div | solution.py:32
  57.0 0.0 copy-done.1
  57.0 3.5 %multiply_convert_fusion = bf16[2,128,4096]{2,1,0:T(8,128)(2,1)S(1)} fusion(f32[2,128,4096]{2,1,0:T(8,128)} %get-tuple-element.10, f32[2,128]{1,0:T(2,128)S(1)} %multiply_add_fusion, f32[4096]{0:T(1024)S(1)} %get-tuple-element.12, f32[2,128]{1,0:T(2,128)S(1)} %get-tuple-element.9, f32[4096]{0:T(1024)S(1)} %get-tuple-element.11, f32[2,128]{1,0:T(2,128)S(1)} %get-tuple-element.8), kind=kLoop, calls=%fused_computation.8 | loop fusion | flops 7340032 | bytes 6327296 | tf_op jit(solution)/shard_map/convert_element_type | solution.py:42
  60.5 3.8 %copy.9 = bf16[2,128,4096]{1,0,2:T(2,128)(2,1)} copy(bf16[2,128,4096]{2,1,0:T(8,128)(2,1)S(1)} %multiply_convert_fusion) | data formatting | bytes 4194304 | tf_op jit(solution)/shard_map/convert_element_type | solution.py:42
  64.2 4.4 %all-to-all-start = ((bf16[2,128,4096]{1,0,2:T(2,128)(2,1)}), bf16[2,128,4096]{1,0,2:T(2,128)(2,1)}, u32[]{:S(2)}, u32[]{:S(2)}) async-start(bf16[2,128,4096]{1,0,2:T(2,128)(2,1)} %copy.9), calls=%async_computation | async-start | bytes 4194304 | tf_op jit(solution)/shard_map/all_to_all | solution.py:48
  68.7 0.0 copy-start
  68.7 0.0 reduce-scatter.2.cloned.1.call-start
  68.7 3.6 %convolution_bitcast_fusion.1 = f32[128,256]{1,0:T(8,128)} fusion(bf16[2,128,4096]{2,1,0:T(8,128)(2,1)S(1)} %multiply_convert_fusion, bf16[2,4096,256]{2,1,0:T(8,128)(2,1)} %param.4), kind=kOutput, calls=%fused_computation.12 | convolution fusion | flops 536870912 | bytes 6422528 | tf_op jit(solution)/shard_map/tqp,tpc->qc/dot_general | solution.py:43
  72.3 0.0 reduce-scatter.2.cloned.1.call-update
  72.3 0.0 copy-done
  72.3 24.2 %all_gather.3 = bf16[512,256]{1,0:T(8,128)(2,1)S(1)} all-gather(bf16[128,256]{1,0:T(8,128)(2,1)S(1)} %copy-done), channel_id=1, replica_groups=mesh['groups'=2,'track'=4,'frame'=4] {'track'}, dimensions={0}, use_global_device_ids=true | all-gather | bytes 327680 | tf_op jit(solution)/shard_map/all_gather | solution.py:45
  96.6 0.0 all-to-all-done
  96.6 4.7 %copy.10 = bf16[2,128,4,1024]{3,1,2,0:T(8,128)(2,1)S(1)} copy(bf16[2,128,4,1024]{1,0,3,2:T(2,128)(2,1)} %bitcast.6) | data formatting | bytes 4194304 | tf_op jit(solution)/shard_map/all_to_all | solution.py:48
  101.3 2.1 %convolution_bitcast_fusion = f32[1024,2,256]{0,2,1:T(8,128)} fusion(bf16[2,512,1024]{2,1,0:T(8,128)(2,1)S(1)} %bitcast.37, bf16[512,256]{1,0:T(8,128)(2,1)S(1)} %all_gather.3), kind=kOutput, calls=%fused_computation.11 | convolution fusion | flops 536870912 | bytes 4456448 | tf_op jit(solution)/shard_map/tqp,qc->ptc/dot_general | solution.py:46
  103.4 4.1 %copy.12 = f32[1024,2,256]{2,1,0:T(2,128)} copy(f32[1024,2,256]{0,2,1:T(8,128)} %convolution_bitcast_fusion) | data formatting | bytes 4194304
  107.5 0.0 reduce-scatter.2.cloned.1.call-done
  (3 shorter events, 0.0 us)
Async XLA Ops:
  7.2 42.8 %all-reduce.2.cloned.1.call-start = ((), (), s32[]{:S(2)}) async-start(), calls=%async_computation.2 | async-start | bytes 131072 | tf_op jit(solution)/shard_map/psum | solution.py:21
  50.0 7.0 %copy-start.1 = (f32[2,2,128]{2,1,0:T(2,128)S(1)}, f32[2,2,128]{2,1,0:T(2,128)}, u32[]{:S(2)}) copy-start(f32[2,2,128]{2,1,0:T(2,128)} %param.7) | copy-start | bytes 6148
  64.2 32.3 %all-to-all-start = ((bf16[2,128,4096]{1,0,2:T(2,128)(2,1)}), bf16[2,128,4096]{1,0,2:T(2,128)(2,1)}, u32[]{:S(2)}, u32[]{:S(2)}) async-start(bf16[2,128,4096]{1,0,2:T(2,128)(2,1)} %copy.9), calls=%async_computation | async-start | bytes 4194304 | tf_op jit(solution)/shard_map/all_to_all | solution.py:48
  68.7 3.6 %copy-start = (bf16[128,256]{1,0:T(8,128)(2,1)S(1)}, bf16[128,256]{1,0:T(8,128)(2,1)}, u32[]{:S(2)}) copy-start(bf16[128,256]{1,0:T(8,128)(2,1)} %all-reduce.2.cloned.1.call-done) | copy-start | bytes 196612
  68.7 38.8 %reduce-scatter.2.cloned.1.call-start = ((), (), s32[]{:S(2)}) async-start(), calls=%async_computation.3 | async-start | bytes 163840 | tf_op jit(solution)/shard_map/reduce_scatter | solution.py:44
Sparse Core Ops, SparseCore 0:
  12.9 37.0 all-reduce.1
  72.4 19.6 reduce-scatter.1
where the time goes:
time: 115 us; the launch traced here: 114 us
  waiting for transfers between devices  36.5 us (32%)
  blocking collectives  24.2 us (21%)
  local copies, waits for them, and re-layouts  16.8 us (15%)
  between operations  14.1 us (12%)
  matrix products  12.7 us (11%)
  other arithmetic  5.55 us (5%)
  starting transfers between devices  4.52 us (4%)
    psum x1, waiting for transfers between devices, on_device(): query_feat = lax.psum(picked.astype(jnp.bfloat16), 'frame')  36.5 us
    all_gather x1, blocking collectives, on_device(): everyone = lax.all_gather(query_feat, 'track', axis=0, tiled=True)  24.2 us
    div x1, matrix products, on_device(): weights = exp_scores / jnp.sum(exp_scores, axis=2, keepdims=True)  7.01 us
    all_to_all x1, local copies, waits for them, and re-layouts, on_device(): lax.all_to_all(cost_grad, 'track', split_axis=2, concat_axis=1, tiled=True)  4.73 us
    all_to_all x1, starting transfers between devices, on_device(): lax.all_to_all(cost_grad, 'track', split_axis=2, concat_axis=1, tiled=True)  4.44 us
    unnamed x5, local copies, waits for them, and re-layouts  4.12 us
    convert_element_type x1, local copies, waits for them, and re-layouts, on_device(): cost_grad = (weights * (grad_x[:, :, None] * coord_x + grad_y[:, :, None]...  3.77 us
    dot_general x1, matrix products, on_device(): jnp.einsum('tqp,tpc->qc', cost_grad, frames, preferred_element_type=jnp.f...  3.56 us
  transfers between devices with their start and end apart: 3, of which 1 were waited for; matrix products, arithmetic and copies ran while one was open for 13% of the time, Pallas kernels for 0%

commit v1 on v0

--- a/solution.py
+++ b/solution.py
@@ -18,7 +18,8 @@
     row_index = jnp.clip(local_index, 0, held_frames - 1) * pixels + query_pixel
     picked = frames.reshape(held_frames * pixels, channels)[row_index]
     picked = jnp.where(inside[:, None], picked.astype(jnp.float32), 0.0)
-    query_feat = lax.psum(picked.astype(jnp.bfloat16), "frame")
+    q_in = picked.astype(jnp.bfloat16)
+    query_feat = lax.all_gather(q_in, axis_name="frame").sum(axis=0)
     score_scale = C ** (-0.5)
     pixel_ids = jnp.arange(pixels)
     coord_x = (pixel_ids % FEAT_W * (2.0 / (FEAT_W - 1)) - 1.0).astype(jnp.float32)

time: 115 us -> 93.4 us (0.81)
  waiting for transfers between devices: 36.5 us -> 0.02 us
  blocking collectives: 24.2 us -> 39.8 us
    psum x1 -> x0, waiting for transfers between devices: 36.5 us -> none  [on_device(): query_feat = lax.psum(picked.astype(jnp.bfloat16), 'frame')]
    all_gather x0 -> x1, blocking collectives: none -> 15.7 us  [on_device(): query_feat = lax.all_gather(q_in, axis_name='frame').sum(axis=0)]
    unnamed x5 -> x3, local copies, waits for them, and re-layouts: 4.12 us -> 4.12 us
  transfers between devices with their start and end apart: 3 -> 2, of which waited for: 1 -> 0; matrix products, arithmetic and copies ran while one was open for 13% -> 16% of each run, Pallas kernels for 0% -> 0%
where the time goes in v1:
time: 93.4 us; the launch traced here: 92.9 us
  blocking collectives  39.8 us (43%)
  local copies, waits for them, and re-layouts  16.9 us (18%)
  between operations  14.1 us (15%)
  matrix products  12.6 us (13%)
  other arithmetic  4.96 us (5%)
  starting transfers between devices  4.48 us (5%)
    all_gather x1, blocking collectives, on_device(): everyone = lax.all_gather(query_feat, 'track', axis=0, tiled=True)  24.1 us
    all_gather x1, blocking collectives, on_device(): query_feat = lax.all_gather(q_in, axis_name='frame').sum(axis=0)  15.7 us
    div x1, matrix products, on_device(): weights = exp_scores / jnp.sum(exp_scores, axis=2, keepdims=True)  6.95 us
    all_to_all x1, local copies, waits for them, and re-layouts, on_device(): lax.all_to_all(cost_grad, 'track', split_axis=2, concat_axis=1, tiled=True)  4.73 us
    all_to_all x1, starting transfers between devices, on_device(): lax.all_to_all(cost_grad, 'track', split_axis=2, concat_axis=1, tiled=True)  4.44 us
    unnamed x3, local copies, waits for them, and re-layouts  4.12 us
    convert_element_type x1, local copies, waits for them, and re-layouts, on_device(): cost_grad = (weights * (grad_x[:, :, None] * coord_x + grad_y[:, :, None]...  3.77 us
    dot_general x1, matrix products, on_device(): jnp.einsum('tqp,tpc->qc', cost_grad, frames, preferred_element_type=jnp.f...  3.56 us
  transfers between devices with their start and end apart: 2, of which 0 were waited for; matrix products, arithmetic and copies ran while one was open for 16% of the time, Pallas kernels for 0%

profile of v1, /device:TPU:0, one launch (start us, length us, event | category | flops | bytes accessed | tf_op | source)
XLA Modules:
  0.0 92.9 jit_solution(8576543731587749341)
XLA Ops:
  7.2 0.7 compare_and_fusion
  7.9 0.7 compare_select_fusion
  8.5 3.5 %gather_fusion = bf16[128,256]{1,0:T(8,128)(2,1)S(1)} fusion(bf16[8192,256]{1,0:T(8,128)(2,1)} %bitcast.41, s32[1024]{0:T(1024)S(1)} %pad_clamp_fusion), kind=kCustom, calls=%fused_computation | custom fusion | bytes 131584 | tf_op jit(solution)/shard_map/gather | solution.py:19
  12.0 0.1 fusion.7
  12.1 15.7 %all_gather.7 = bf16[4,128,256]{2,1,0:T(8,128)(2,1)S(1)} all-gather(bf16[1,128,256]{2,1,0:T(8,128)(2,1)S(1)} %fusion.7), channel_id=1, replica_groups=mesh['groups'=2,'track'=4,'frame'=4] {'frame'}, dimensions={0}, use_global_device_ids=true | all-gather | bytes 327680 | tf_op jit(solution)/shard_map/all_gather | solution.py:22
  27.8 0.7 slice_bitcast_fusion.1
  28.5 0.0 copy-start
  28.5 7.0 %multiply_reduce_fusion.1 = (f32[2,128]{1,0:T(2,128)S(1)}, f32[2,128]{1,0:T(2,128)S(1)}, f32[2,128,4096]{2,1,0:T(8,128)}) fusion(f32[4096]{0:T(1024)S(1)} %get-tuple-element.11, f32[4096]{0:T(1024)S(1)} %get-tuple-element.12, bf16[2,4096,256]{2,1,0:T(8,128)(2,1)} %param.4, bf16[128,256]{1,0:T(8,128)(2,1)S(1)} %reduce_sum.39), kind=kOutput, calls=%fused_computation.10 | convolution fusion | flops 544219136 | bytes 8488960 | tf_op jit(solution)/shard_map/div | solution.py:33
  35.5 0.0 copy-done
  35.5 3.5 %multiply_convert_fusion = bf16[2,128,4096]{2,1,0:T(8,128)(2,1)S(1)} fusion(f32[2,128,4096]{2,1,0:T(8,128)} %get-tuple-element.10, f32[2,128]{1,0:T(2,128)S(1)} %multiply_add_fusion, f32[4096]{0:T(1024)S(1)} %get-tuple-element.12, f32[2,128]{1,0:T(2,128)S(1)} %get-tuple-element.9, f32[4096]{0:T(1024)S(1)} %get-tuple-element.11, f32[2,128]{1,0:T(2,128)S(1)} %get-tuple-element.8), kind=kLoop, calls=%fused_computation.8 | loop fusion | flops 7340032 | bytes 6327296 | tf_op jit(solution)/shard_map/convert_element_type | solution.py:43
  39.0 3.8 %copy.10 = bf16[2,128,4096]{1,0,2:T(2,128)(2,1)} copy(bf16[2,128,4096]{2,1,0:T(8,128)(2,1)S(1)} %multiply_convert_fusion) | data formatting | bytes 4194304 | tf_op jit(solution)/shard_map/convert_element_type | solution.py:43
  42.7 4.4 %all-to-all-start = ((bf16[2,128,4096]{1,0,2:T(2,128)(2,1)}), bf16[2,128,4096]{1,0,2:T(2,128)(2,1)}, u32[]{:S(2)}, u32[]{:S(2)}) async-start(bf16[2,128,4096]{1,0,2:T(2,128)(2,1)} %copy.10), calls=%async_computation | async-start | bytes 4194304 | tf_op jit(solution)/shard_map/all_to_all | solution.py:49
  47.2 0.0 reduce-scatter.2.cloned.1.call-start
  47.2 3.6 %convolution_bitcast_fusion.1 = f32[128,256]{1,0:T(8,128)} fusion(bf16[2,128,4096]{2,1,0:T(8,128)(2,1)S(1)} %multiply_convert_fusion, bf16[2,4096,256]{2,1,0:T(8,128)(2,1)} %param.4), kind=kOutput, calls=%fused_computation.12 | convolution fusion | flops 536870912 | bytes 6422528 | tf_op jit(solution)/shard_map/tqp,tpc->qc/dot_general | solution.py:44
  50.8 0.0 reduce-scatter.2.cloned.1.call-update
  50.8 0.1 copy.9
  50.9 24.1 %all_gather.8 = bf16[512,256]{0,1:T(8,128)(2,1)S(1)} all-gather(bf16[128,256]{0,1:T(8,128)(2,1)S(1)} %copy.9), channel_id=1, replica_groups=mesh['groups'=2,'track'=4,'frame'=4] {'track'}, dimensions={0}, use_global_device_ids=true | all-gather | bytes 327680 | tf_op jit(solution)/shard_map/all_gather | solution.py:46
  75.1 0.0 all-to-all-done
  75.1 4.7 %copy.11 = bf16[2,128,4,1024]{3,1,2,0:T(8,128)(2,1)S(1)} copy(bf16[2,128,4,1024]{1,0,3,2:T(2,128)(2,1)} %bitcast.7) | data formatting | bytes 4194304 | tf_op jit(solution)/shard_map/all_to_all | solution.py:49
  79.8 2.1 %convolution_bitcast_fusion = f32[1024,2,256]{0,2,1:T(8,128)} fusion(bf16[2,512,1024]{2,1,0:T(8,128)(2,1)S(1)} %bitcast.40, bf16[512,256]{0,1:T(8,128)(2,1)S(1)} %all_gather.8), kind=kOutput, calls=%fused_computation.11 | convolution fusion | flops 536870912 | bytes 4456448 | tf_op jit(solution)/shard_map/tqp,qc->ptc/dot_general | solution.py:47
  81.9 4.1 %copy.12 = f32[1024,2,256]{2,1,0:T(2,128)} copy(f32[1024,2,256]{0,2,1:T(8,128)} %convolution_bitcast_fusion) | data formatting | bytes 4194304
  86.0 0.0 reduce-scatter.2.cloned.1.call-done
  (4 shorter events, 0.1 us)
Async XLA Ops:
  28.5 7.0 %copy-start = (f32[2,2,128]{2,1,0:T(2,128)S(1)}, f32[2,2,128]{2,1,0:T(2,128)}, u32[]{:S(2)}) copy-start(f32[2,2,128]{2,1,0:T(2,128)} %param.7) | copy-start | bytes 6148
  42.7 32.4 %all-to-all-start = ((bf16[2,128,4096]{1,0,2:T(2,128)(2,1)}), bf16[2,128,4096]{1,0,2:T(2,128)(2,1)}, u32[]{:S(2)}, u32[]{:S(2)}) async-start(bf16[2,128,4096]{1,0,2:T(2,128)(2,1)} %copy.10), calls=%async_computation | async-start | bytes 4194304 | tf_op jit(solution)/shard_map/all_to_all | solution.py:49
  47.2 38.8 %reduce-scatter.2.cloned.1.call-start = ((), (), s32[]{:S(2)}) async-start(), calls=%async_computation.2 | async-start | bytes 163840 | tf_op jit(solution)/shard_map/reduce_scatter | solution.py:45
Sparse Core Ops, SparseCore 0:
  50.9 21.4 reduce-scatter.1
